TPU v7x, 32 devices: a whole 2x2x4 slice. The times are simulated.
32 devices in a mesh: wide: 8 (over z, x), tensor: 4 (over y, core).
Axes of the slice: x: 2, y: 2, z: 4, core: 2. Of those that a mesh axis runs over, the one named last changes fastest.
Arguments:
- tokens: bfloat16 [2, 12544, 768], P(None, ('wide', 'tensor')), may hold values from -6 to 6
- cotangent: bfloat16 [2, 12544, 768], P(None, ('wide', 'tensor')), may hold values from -6 to 6
- ln_gain: bfloat16 [3, 768], P(None, 'wide'), may hold values from 0.25 to 1.75
- biases: bfloat16 [10, 768], P(None, 'wide'), may hold values from -1.1953125 to 1.1953125
- fc1_bias: bfloat16 [3072], P('wide'), may hold values from -1.1953125 to 1.1953125
- w_qkv_s: bfloat16 [3, 768, 768], P(None, 'wide', 'tensor'), may hold values from -0.21875 to 0.21875
- w_out_s: bfloat16 [768, 768], P('tensor', 'wide'), may hold values from -2.5 to 2.5
- w_qkv_t: bfloat16 [3, 768, 768], P(None, 'wide', 'tensor'), may hold values from -0.21875 to 0.21875
- w_out_t: bfloat16 [768, 768], P('tensor', 'wide'), may hold values from -0.625 to 0.625
- w_up: bfloat16 [768, 3072], P('wide', 'tensor'), may hold values from -0.21875 to 0.21875
- w_down: bfloat16 [3072, 768], P('tensor', 'wide'), may hold values from -0.109375 to 0.109375
Outputs:
- mixed: bfloat16 [2, 12544, 768], P(None, ('wide', 'tensor'))
- grad_tokens: float32 [2, 12544, 768], P(None, ('wide', 'tensor'))
- grad_ln_gain: float32 [3, 768], P(None, 'wide')
- grad_biases: float32 [10, 768], P(None, 'wide')
- grad_fc1_bias: float32 [3072], P('wide')
- grad_w_qkv_s: float32 [3, 768, 768], P(None, 'wide', 'tensor')
- grad_w_out_s: float32 [768, 768], P('tensor', 'wide')
- grad_w_qkv_t: float32 [3, 768, 768], P(None, 'wide', 'tensor')
- grad_w_out_t: float32 [768, 768], P('tensor', 'wide')
- grad_w_up: float32 [768, 3072], P('wide', 'tensor')
- grad_w_down: float32 [3072, 768], P('tensor', 'wide')
All inputs are finite; a program needn't handle non-finite values.
Results may differ from a plain program's by a relative error of at most 0.014.
Values may be sent and summed in bfloat16 or wider, within the bound.
No kernel may reach another device: no remote copies, remote signals or barrier semaphores. Data moves between devices by JAX's collectives and lax.ppermute only.
A program may use at most 256 MiB of HBM per device.

v0:
```python
import jax
import jax.numpy as jnp
from jax import lax
from jax.sharding import PartitionSpec as P

HEAD_DIM = 64
PATCHES = 196
FRAMES = 16
FRAME_RUN = 2
EPSILON = 1e-06


def layer_norm(rows, gain, shift):
    center = rows - jnp.mean(rows, axis=-1, keepdims=True)
    spread = jnp.mean(center * center, axis=-1, keepdims=True)
    return center * lax.rsqrt(spread + EPSILON) * gain + shift


def exact_gelu(values):
    return jax.nn.gelu(values, approximate=False)


def norm_back(rows_in, gain, shift, grad_rows):
    _, pullback = jax.vjp(layer_norm, rows_in, gain, shift)
    return pullback(grad_rows)


def into_time(block, clip_count):
    rest = block.shape[1:]
    grouped = block.reshape((FRAMES // FRAME_RUN, clip_count, FRAME_RUN) + rest)
    return jnp.swapaxes(grouped, 1, 2).reshape((FRAMES, clip_count) + rest)


def out_of_time(block):
    clip_count = block.shape[1]
    rest = block.shape[2:]
    grouped = block.reshape((FRAMES // FRAME_RUN, FRAME_RUN, clip_count) + rest)
    return jnp.swapaxes(grouped, 1, 2).reshape((FRAMES * clip_count,) + rest)


def attend(queries, key_rows, value_rows, einsum_forms):
    score_form, out_form, key_form = einsum_forms
    score_scale = queries.shape[-1] ** (-0.5)
    scores = (
        jnp.einsum(score_form, queries, key_rows, preferred_element_type=jnp.float32) * score_scale
    )
    log_total = jax.nn.logsumexp(scores, axis=-1, keepdims=True)
    weights = jnp.exp(scores - log_total).astype(jnp.bfloat16)
    result = jnp.einsum(out_form, weights, value_rows, preferred_element_type=jnp.float32)
    return (result.astype(jnp.bfloat16), log_total)


def attend_back(queries, key_rows, value_rows, log_total, grad_out, einsum_forms):
    score_form, out_form, key_form = einsum_forms
    score_scale = queries.shape[-1] ** (-0.5)
    scores = (
        jnp.einsum(score_form, queries, key_rows, preferred_element_type=jnp.float32) * score_scale
    )
    probabilities = jnp.exp(scores - log_total)
    grad_probs = jnp.einsum(score_form, grad_out, value_rows, preferred_element_type=jnp.float32)
    row_inner = jnp.sum(probabilities * grad_probs, axis=-1, keepdims=True)
    grad_scores = (probabilities * (grad_probs - row_inner)).astype(jnp.bfloat16)
    grad_q = (
        jnp.einsum(out_form, grad_scores, key_rows, preferred_element_type=jnp.float32)
        * score_scale
    ).astype(jnp.bfloat16)
    grad_k = (
        jnp.einsum(key_form, grad_scores, queries, preferred_element_type=jnp.float32) * score_scale
    ).astype(jnp.bfloat16)
    grad_v = jnp.einsum(
        key_form, probabilities.astype(jnp.bfloat16), grad_out, preferred_element_type=jnp.float32
    ).astype(jnp.bfloat16)
    return (grad_q, grad_k, grad_v)


def product_term(einsum_form, left, right):

    def term(first_row, row_span):
        return jnp.einsum(einsum_form, left, right, preferred_element_type=jnp.float32)

    return term


def gather_rows(block):
    return lax.all_gather(block, "tensor", axis=0, tiled=True)


def sum_rows(term, row_count):
    return lax.psum_scatter(
        term(jnp.int32(0), row_count * lax.axis_size("tensor")),
        "tensor",
        scatter_dimension=0,
        tiled=True,
    )


def out_project(attn_rows, w_out_piece, row_count):
    return sum_rows(product_term("gc,cd->gd", attn_rows, w_out_piece), row_count)


def to_patches(block, patch_pad):
    padded = jnp.pad(block, ((0, 0), (0, patch_pad - block.shape[1]), (0, 0)))
    return lax.all_to_all(padded, "wide", split_axis=1, concat_axis=0, tiled=True)


def to_frames(block, patch_count):
    returned = lax.all_to_all(block, "wide", split_axis=0, concat_axis=1, tiled=True)
    return returned[:, :patch_count]


def reduce_wide(packed):
    return (
        lax.psum_scatter(packed[0], "wide", scatter_dimension=1, tiled=True),
        lax.psum_scatter(packed[1], "wide", scatter_dimension=1, tiled=True),
        lax.psum_scatter(packed[2], "wide", scatter_dimension=1, tiled=True),
        lax.psum_scatter(packed[3], "wide", scatter_dimension=1, tiled=True),
        lax.psum_scatter(packed[4], "wide", scatter_dimension=0, tiled=True),
        lax.psum_scatter(packed[5], "wide", scatter_dimension=1, tiled=True),
        lax.psum_scatter(packed[6], "wide", scatter_dimension=1, tiled=True),
        lax.psum_scatter(packed[7], "wide", scatter_dimension=1, tiled=True),
        lax.psum_scatter(packed[8], "wide", scatter_dimension=0, tiled=True),
    )


def per_device(
    tokens, cotangent, ln_gain, biases, fc1_bias, w_qkv_s, w_out_s, w_qkv_t, w_out_t, w_up, w_down
):
    wide_count = lax.axis_size("wide")
    tensor_count = lax.axis_size("tensor")
    tensor_rank = lax.axis_index("tensor")
    micro_total = tokens.shape[0]
    row_count = tokens.shape[1]
    model_width = tokens.shape[2]
    head_cols = w_qkv_s.shape[2]
    hidden = w_up.shape[1]
    local_heads = head_cols // HEAD_DIM
    frames = row_count * tensor_count // PATCHES
    patch_slot = (PATCHES + wide_count - 1) // wide_count
    patch_pad = patch_slot * wide_count
    clip_count = frames * wide_count // FRAMES
    spatial_forms = ("fphe,fqhe->fhpq", "fhpq,fqhe->fphe", "fhpq,fphe->fqhe")
    temporal_forms = ("tcphe,ucphe->cphtu", "cphtu,ucphe->tcphe", "cphtu,tcphe->ucphe")

    def fetch_all():
        return (
            lax.all_gather(w_qkv_s, "wide", axis=1, tiled=True),
            lax.all_gather(w_out_s, "wide", axis=1, tiled=True),
            lax.all_gather(w_qkv_t, "wide", axis=1, tiled=True),
            lax.all_gather(w_out_t, "wide", axis=1, tiled=True),
            lax.all_gather(w_up, "wide", axis=0, tiled=True),
            lax.all_gather(w_down, "wide", axis=1, tiled=True),
            lax.all_gather(ln_gain, "wide", axis=1, tiled=True),
            lax.all_gather(biases, "wide", axis=1, tiled=True),
            lax.all_gather(fc1_bias, "wide", axis=0, tiled=True),
        )

    shares = None
    sums = [
        jnp.zeros((3, model_width, head_cols), jnp.float32),
        jnp.zeros((head_cols, model_width), jnp.float32),
        jnp.zeros((3, model_width, head_cols), jnp.float32),
        jnp.zeros((head_cols, model_width), jnp.float32),
        jnp.zeros((model_width, hidden), jnp.float32),
        jnp.zeros((hidden, model_width), jnp.float32),
        jnp.zeros((3, model_width), jnp.float32),
        jnp.zeros((10, model_width), jnp.float32),
        jnp.zeros((3, head_cols), jnp.float32),
        jnp.zeros((3, head_cols), jnp.float32),
        jnp.zeros((hidden,), jnp.float32),
    ]
    outputs = []
    input_grads = []
    for micro_index in range(micro_total):
        fetched = fetch_all()
        gains = fetched[6].astype(jnp.float32)
        shifts = fetched[7].astype(jnp.float32)
        offset = tensor_rank * head_cols
        empty_cols = jnp.zeros((head_cols,), jnp.float32)
        bias_s = jnp.stack(
            [
                lax.dynamic_slice_in_dim(shifts[3], offset, head_cols),
                empty_cols,
                lax.dynamic_slice_in_dim(shifts[4], offset, head_cols),
            ]
        )
        bias_t = jnp.stack(
            [
                lax.dynamic_slice_in_dim(shifts[6], offset, head_cols),
                empty_cols,
                lax.dynamic_slice_in_dim(shifts[7], offset, head_cols),
            ]
        )
        up_bias = lax.dynamic_slice_in_dim(
            fetched[8].astype(jnp.float32), tensor_rank * hidden, hidden
        )
        gains, shifts, bias_s, bias_t, up_bias = (gains, shifts, bias_s, bias_t, up_bias)
        source = tokens[micro_index].astype(jnp.float32)
        norm_s = layer_norm(source, gains[0], shifts[0]).astype(jnp.bfloat16)
        full_s = gather_rows(norm_s)
        qkv_s = (
            jnp.einsum("gd,kdc->gkc", full_s, fetched[0], preferred_element_type=jnp.float32)
            + bias_s
        ).astype(jnp.bfloat16)
        split_s = qkv_s.reshape(frames, PATCHES, 3, local_heads, HEAD_DIM)
        attn_s, total_s = attend(
            split_s[:, :, 0], split_s[:, :, 1], split_s[:, :, 2], spatial_forms
        )
        attn_s = attn_s.reshape(-1, head_cols)
        resid_s = source + out_project(attn_s, fetched[1], row_count) + shifts[5]
        norm_t = layer_norm(resid_s, gains[1], shifts[1]).astype(jnp.bfloat16)
        full_t = gather_rows(norm_t)
        qkv_t = (
            jnp.einsum("gd,kdc->gkc", full_t, fetched[2], preferred_element_type=jnp.float32)
            + bias_t
        ).astype(jnp.bfloat16)
        moved = to_patches(qkv_t.reshape(frames, PATCHES, 3 * head_cols), patch_pad)
        split_t = into_time(moved, clip_count).reshape(
            FRAMES, clip_count, patch_slot, 3, local_heads, HEAD_DIM
        )
        attn_t, total_t = attend(
            split_t[:, :, :, 0], split_t[:, :, :, 1], split_t[:, :, :, 2], temporal_forms
        )
        attn_t = out_of_time(attn_t).reshape(wide_count * frames, patch_slot, head_cols)
        attn_t = to_frames(attn_t, PATCHES).reshape(-1, head_cols)
        resid_t = resid_s + out_project(attn_t, fetched[3], row_count) + shifts[8]
        norm_m = layer_norm(resid_t, gains[2], shifts[2]).astype(jnp.bfloat16)
        full_m = gather_rows(norm_m)
        pre_act = jnp.dot(full_m, fetched[4], preferred_element_type=jnp.float32) + up_bias
        activ = exact_gelu(pre_act).astype(jnp.bfloat16)
        mixed_rows = (
            resid_t + sum_rows(product_term("gf,fd->gd", activ, fetched[5]), row_count) + shifts[9]
        )
        outputs.append(mixed_rows.astype(jnp.bfloat16))
        fetched = fetch_all()
        grad_out = cotangent[micro_index].astype(jnp.float32)
        sums[7] = sums[7].at[9].add(jnp.sum(grad_out, axis=0))
        grad_branch = gather_rows(grad_out.astype(jnp.bfloat16))
        sums[5] = sums[5] + jnp.einsum(
            "gf,gd->fd", activ, grad_branch, preferred_element_type=jnp.float32
        )
        grad_act = jnp.einsum(
            "gd,fd->gf", grad_branch, fetched[5], preferred_element_type=jnp.float32
        )
        _, gelu_pull = jax.vjp(exact_gelu, pre_act)
        grad_pre = gelu_pull(grad_act)[0].astype(jnp.bfloat16)
        sums[4] = sums[4] + jnp.einsum(
            "gd,gf->df", full_m, grad_pre, preferred_element_type=jnp.float32
        )
        sums[10] = sums[10] + jnp.sum(grad_pre, axis=0, dtype=jnp.float32)
        grad_norm = sum_rows(product_term("gf,df->gd", grad_pre, fetched[4]), row_count)
        back_in, back_gain, back_shift = norm_back(resid_t, gains[2], shifts[2], grad_norm)
        sums[6] = sums[6].at[2].add(back_gain)
        sums[7] = sums[7].at[2].add(back_shift)
        grad_resid = grad_out + back_in
        sums[7] = sums[7].at[8].add(jnp.sum(grad_resid, axis=0))
        grad_branch = gather_rows(grad_resid.astype(jnp.bfloat16))
        sums[3] = sums[3] + jnp.einsum(
            "gc,gd->cd", attn_t, grad_branch, preferred_element_type=jnp.float32
        )
        grad_attn = jnp.einsum(
            "gd,cd->gc", grad_branch, fetched[3], preferred_element_type=jnp.float32
        ).astype(jnp.bfloat16)
        grad_moved = to_patches(grad_attn.reshape(frames, PATCHES, head_cols), patch_pad)
        grad_moved = into_time(grad_moved, clip_count).reshape(
            FRAMES, clip_count, patch_slot, local_heads, HEAD_DIM
        )
        grad_q, grad_k, grad_v = attend_back(
            split_t[:, :, :, 0],
            split_t[:, :, :, 1],
            split_t[:, :, :, 2],
            total_t,
            grad_moved,
            temporal_forms,
        )
        grad_qkv = out_of_time(jnp.stack([grad_q, grad_k, grad_v], axis=3)).reshape(
            wide_count * frames, patch_slot, 3 * head_cols
        )
        grad_qkv = to_frames(grad_qkv, PATCHES).reshape(-1, 3, head_cols)
        sums[2] = sums[2] + jnp.einsum(
            "gd,gkc->kdc", full_t, grad_qkv, preferred_element_type=jnp.float32
        )
        sums[9] = sums[9] + jnp.sum(grad_qkv, axis=0, dtype=jnp.float32)
        grad_norm = sum_rows(product_term("gkc,kdc->gd", grad_qkv, fetched[2]), row_count)
        back_in, back_gain, back_shift = norm_back(resid_s, gains[1], shifts[1], grad_norm)
        sums[6] = sums[6].at[1].add(back_gain)
        sums[7] = sums[7].at[1].add(back_shift)
        grad_resid = grad_resid + back_in
        sums[7] = sums[7].at[5].add(jnp.sum(grad_resid, axis=0))
        grad_branch = gather_rows(grad_resid.astype(jnp.bfloat16))
        sums[1] = sums[1] + jnp.einsum(
            "gc,gd->cd", attn_s, grad_branch, preferred_element_type=jnp.float32
        )
        grad_attn = jnp.einsum(
            "gd,cd->gc", grad_branch, fetched[1], preferred_element_type=jnp.float32
        ).astype(jnp.bfloat16)
        grad_heads = grad_attn.reshape(frames, PATCHES, local_heads, HEAD_DIM)
        grad_q, grad_k, grad_v = attend_back(
            split_s[:, :, 0], split_s[:, :, 1], split_s[:, :, 2], total_s, grad_heads, spatial_forms
        )
        grad_qkv = jnp.stack([grad_q, grad_k, grad_v], axis=2).reshape(-1, 3, head_cols)
        sums[0] = sums[0] + jnp.einsum(
            "gd,gkc->kdc", full_s, grad_qkv, preferred_element_type=jnp.float32
        )
        sums[8] = sums[8] + jnp.sum(grad_qkv, axis=0, dtype=jnp.float32)
        grad_norm = sum_rows(product_term("gkc,kdc->gd", grad_qkv, fetched[0]), row_count)
        back_in, back_gain, back_shift = norm_back(source, gains[0], shifts[0], grad_norm)
        sums[6] = sums[6].at[0].add(back_gain)
        sums[7] = sums[7].at[0].add(back_shift)
        input_grads.append(grad_resid + back_in)
    columns = jnp.stack([sums[8][0], sums[8][2], sums[9][0], sums[9][2]])
    placed = lax.dynamic_update_slice(
        jnp.zeros((4, model_width), jnp.float32), columns, (0, tensor_rank * head_cols)
    )
    blank = jnp.zeros((1, model_width), jnp.float32)
    shift_full = sums[7] + jnp.concatenate(
        [blank, blank, blank, placed[0:2], blank, placed[2:4], blank, blank], axis=0
    )
    up_full = lax.dynamic_update_slice(
        jnp.zeros((hidden * tensor_count,), jnp.float32), sums[10], (tensor_rank * hidden,)
    )
    shares = reduce_wide(
        (sums[0], sums[1], sums[2], sums[3], sums[4], sums[5], sums[6], shift_full, up_full)
    )
    gain_grad, shift_grad, up_grad = lax.psum((shares[6], shares[7], shares[8]), "tensor")
    return (
        jnp.stack(outputs),
        jnp.stack(input_grads),
        gain_grad,
        shift_grad,
        up_grad,
        shares[0],
        shares[1],
        shares[2],
        shares[3],
        shares[4],
        shares[5],
    )


def solution(mesh):
    return jax.shard_map(
        per_device,
        mesh=mesh,
        in_specs=(
            P(None, ("wide", "tensor"), None),
            P(None, ("wide", "tensor"), None),
            P(None, "wide"),
            P(None, "wide"),
            P("wide"),
            P(None, "wide", "tensor"),
            P("tensor", "wide"),
            P(None, "wide", "tensor"),
            P("tensor", "wide"),
            P("wide", "tensor"),
            P("tensor", "wide"),
        ),
        out_specs=(
            P(None, ("wide", "tensor"), None),
            P(None, ("wide", "tensor"), None),
            P(None, "wide"),
            P(None, "wide"),
            P("wide"),
            P(None, "wide", "tensor"),
            P("tensor", "wide"),
            P(None, "wide", "tensor"),
            P("tensor", "wide"),
            P("wide", "tensor"),
            P("tensor", "wide"),
        ),
        check_vma=False,
    )
```

profile of v0, /device:TPU:0, one launch (start us, length us, event | category | flops | bytes accessed | tf_op | source)
XLA Modules:
  0.0 2080.9 jit_solution(17069805705926739419)
XLA Ops:
  8.1 32.7 %all-gather.3 = bf16[8,96,10]{1,2,0:T(8,128)(2,1)S(1)} all-gather(bf16[1,96,10]{1,2,0:T(8,128)(2,1)} %bitcast.574), channel_id=1, replica_groups=mesh['wide'=8,'tensor'=4] {'wide'}, dimensions={0}, use_global_device_ids=true | all-gather | bytes 17280 | tf_op jit(solution)/shard_map/all_gather | solution.py:153
  45.4 20.5 all-gather.2
  68.6 35.7 %all_gather.87 = bf16[3,768,192]{2,0,1:T(4,128)(2,1)} all-gather(bf16[3,96,192]{2,0,1:T(4,128)(2,1)S(1)} %copy.214), channel_id=1, replica_groups=mesh['wide'=8,'tensor'=4] {'wide'}, dimensions={1}, use_global_device_ids=true | all-gather | bytes 995328 | tf_op jit(solution)/shard_map/all_gather | solution.py:146
  107.2 31.2 %all_gather.88 = bf16[192,768]{0,1:T(8,128)(2,1)S(1)} all-gather(bf16[192,96]{0,1:T(8,128)(2,1)S(1)} %copy.221), channel_id=1, replica_groups=mesh['wide'=8,'tensor'=4] {'wide'}, dimensions={1}, use_global_device_ids=true | all-gather | bytes 331776 | tf_op jit(solution)/shard_map/all_gather | solution.py:147
  185.0 29.6 %reduce-scatter.39.cloned.1.call-done = f32[392,768]{1,0:T(8,128)} async-done(((f32[1568,768]{1,0:T(8,128)}), f32[392,768]{1,0:T(8,128)}) %reduce-scatter.39.cloned.1.call-update) | async-done | bytes 1204240 | tf_op jit(solution)/shard_map/reduce_scatter | solution.py:89
  214.5 51.0 %reduce-scatter.33.cloned.1.call-done = f32[392,768]{1,0:T(8,128)} async-done(((f32[1568,768]{1,0:T(8,128)}), f32[392,768]{1,0:T(8,128)}) %reduce-scatter.33.cloned.1.call-update) | async-done | bytes 1204240 | tf_op jit(solution)/shard_map/reduce_scatter | solution.py:89
  271.9 37.6 %all_gather.90 = bf16[3,768,192]{2,0,1:T(4,128)(2,1)S(1)} all-gather(bf16[3,96,192]{2,0,1:T(4,128)(2,1)S(1)} %copy.222), channel_id=1, replica_groups=mesh['wide'=8,'tensor'=4] {'wide'}, dimensions={1}, use_global_device_ids=true | all-gather | bytes 995328 | tf_op jit(solution)/shard_map/all_gather | solution.py:148
  331.7 6.5 copy.339
  338.4 53.1 %all_to_all.132 = bf16[8,200,576]{2,0,1:T(8,128)(2,1)S(1)} all-to-all(bf16[8,200,576]{2,0,1:T(8,128)(2,1)S(1)} %pad.53.clone), channel_id=1, replica_groups=mesh['wide'=8,'tensor'=4] {'wide'}, dimensions={1} | all-to-all | bytes 3686400 | tf_op jit(solution)/shard_map/all_to_all | solution.py:103
  417.5 46.3 %all_gather.91 = bf16[192,768]{0,1:T(8,128)(2,1)S(1)} all-gather(bf16[192,96]{0,1:T(8,128)(2,1)S(1)} %copy.234), channel_id=1, replica_groups=mesh['wide'=8,'tensor'=4] {'wide'}, dimensions={1}, use_global_device_ids=true | all-gather | bytes 331776 | tf_op jit(solution)/shard_map/all_gather | solution.py:149
  485.0 46.4 %all_to_all.133 = bf16[8,200,576]{2,0,1:T(8,128)(2,1)} all-to-all(bf16[8,200,576]{2,0,1:T(8,128)(2,1)S(1)} %pad.52.clone), channel_id=1, replica_groups=mesh['wide'=8,'tensor'=4] {'wide'}, dimensions={1} | all-to-all | bytes 3686400 | tf_op jit(solution)/shard_map/all_to_all | solution.py:103
  540.2 10.0 reshape_reshape.24
  564.9 27.2 %all_to_all.134 = bf16[64,25,192]{2,1,0:T(8,128)(2,1)S(1)} all-to-all(bf16[64,25,192]{2,1,0:T(8,128)(2,1)S(1)} %copy.231), channel_id=1, replica_groups=mesh['wide'=8,'tensor'=4] {'wide'}, dimensions={0} | all-to-all | bytes 1228800 | tf_op jit(solution)/shard_map/all_to_all | solution.py:107
  602.2 46.2 %reduce-scatter.35.cloned.1.call-done = f32[392,768]{1,0:T(8,128)} async-done(((f32[1568,768]{1,0:T(8,128)}), f32[392,768]{1,0:T(8,128)}) %reduce-scatter.35.cloned.1.call-update) | async-done | bytes 1204240 | tf_op jit(solution)/shard_map/reduce_scatter | solution.py:89
  655.8 26.3 %all-gather.4 = bf16[8,1,384]{2,1,0:T(2,128)(2,1)S(1)} all-gather(bf16[1,1,384]{2,1,0:T(2,128)(2,1)S(1)} %reshape.852), channel_id=1, replica_groups=mesh['wide'=8,'tensor'=4] {'wide'}, dimensions={0}, use_global_device_ids=true | all-gather | bytes 6912 | tf_op jit(solution)/shard_map/all_gather | solution.py:154
  682.2 6.3 fusion.158
  688.5 14.5 all-gather.24.cloned.1.call-done
  703.0 24.7 %multiply_convert_fusion.3 = (bf16[1568,768]{1,0:T(8,128)(2,1)}, f32[1568,768]{1,0:T(8,128)}, bf16[1568,768]{1,0:T(8,128)(2,1)}, f32[1568,768]{1,0:T(8,128)}, f32[1568,768]{1,0:T(8,128)}) fusion(f32[768]{0:T(1024)S(1)} %dynamic_slice.24, f32[1568,768]{1,0:T(8,128)} %fusion.158, bf16[1568,768]{1,0:T(8,128)(2,1)} %all-gather.24.cloned.1.call-done, ...), kind=kOutput, calls=%fused_computation.31 | convolution fusion | flops 2008645632 | bytes 27675648 | tf_op jit(solution)/shard_map/dot_general | solution.py:228
  727.8 18.9 all-gather.28.cloned.1.call-done
  746.7 24.2 %all-gather.46.cloned.1.call-done = bf16[1,1568,768]{2,1,0:T(8,128)(2,1)} async-done(((bf16[1,392,768]{2,1,0:T(8,128)(2,1)}), bf16[1,1568,768]{2,1,0:T(8,128)(2,1)}) %all-gather.46.cloned.1.call-update) | async-done | bytes 2408464 | tf_op jit(solution)/shard_map/all_gather | solution.py:85
  770.9 8.9 convert_reduce_fusion
  785.7 10.9 all-gather.44.cloned.1.call-done
  796.7 8.1 convert_reduce_fusion.1
  822.7 24.8 %reduce-scatter.51.cloned.1.call-done = f32[392,768]{1,0:T(8,128)} async-done(((f32[1568,768]{1,0:T(8,128)}), f32[392,768]{1,0:T(8,128)}) %reduce-scatter.51.cloned.1.call-update) | async-done | bytes 1204240 | tf_op jit(solution)/shard_map/reduce_scatter | solution.py:89
  847.6 50.9 %reduce-scatter.45.cloned.1.call-done = f32[392,768]{1,0:T(8,128)} async-done(((f32[1568,768]{1,0:T(8,128)}), f32[392,768]{1,0:T(8,128)}) %reduce-scatter.45.cloned.1.call-update) | async-done | bytes 1204240 | tf_op jit(solution)/shard_map/reduce_scatter | solution.py:89
  901.1 48.3 %reduce-scatter.37.cloned.1.call-done = f32[392,768]{1,0:T(8,128)} async-done(((f32[1568,768]{1,0:T(8,128)}), f32[392,768]{1,0:T(8,128)}) %reduce-scatter.37.cloned.1.call-update) | async-done | bytes 1204240 | tf_op jit(solution)/shard_map/reduce_scatter | solution.py:89
  949.4 51.1 %reduce-scatter.43.cloned.1.call-done = f32[392,768]{1,0:T(8,128)} async-done(((f32[1568,768]{1,0:T(8,128)}), f32[392,768]{1,0:T(8,128)}) %reduce-scatter.43.cloned.1.call-update) | async-done | bytes 1204240 | tf_op jit(solution)/shard_map/reduce_scatter | solution.py:89
  1007.0 24.5 %all-gather.40.cloned.1.call-done = bf16[1568,768]{1,0:T(8,128)(2,1)} async-done(((bf16[392,768]{1,0:T(8,128)(2,1)}), bf16[1568,768]{1,0:T(8,128)(2,1)}) %all-gather.40.cloned.1.call-update) | async-done | bytes 2408464 | tf_op jit(solution)/shard_map/all_gather | solution.py:85
  1036.7 27.7 %all_to_all.135 = bf16[8,200,192]{2,0,1:T(8,128)(2,1)S(1)} all-to-all(bf16[8,200,192]{2,0,1:T(8,128)(2,1)S(1)} %pad.55), channel_id=1, replica_groups=mesh['wide'=8,'tensor'=4] {'wide'}, dimensions={1} | all-to-all | bytes 1228800 | tf_op jit(solution)/shard_map/all_to_all | solution.py:103
  1088.7 8.1 reshape_reshape.31
  1103.9 57.9 %all-to-all-done.7 = bf16[64,25,576]{2,1,0:T(8,128)(2,1)S(1)} async-done(((bf16[64,25,576]{2,1,0:T(8,128)(2,1)}), bf16[64,25,576]{2,1,0:T(8,128)(2,1)S(1)}, u32[]{:S(2)}, u32[]{:S(2)}) %all-to-all-start.7) | async-done | bytes 1843232 | tf_op jit(solution)/shard_map/all_to_all | solution.py:107
  1184.6 25.4 %all_to_all.136 = bf16[8,200,192]{2,0,1:T(8,128)(2,1)S(1)} all-to-all(bf16[8,200,192]{2,0,1:T(8,128)(2,1)S(1)} %pad.54), channel_id=1, replica_groups=mesh['wide'=8,'tensor'=4] {'wide'}, dimensions={1} | all-to-all | bytes 1228800 | tf_op jit(solution)/shard_map/all_to_all | solution.py:103
  1230.7 8.1 reshape_reshape.29
  1240.0 62.3 %all_to_all.137 = bf16[64,25,576]{2,1,0:T(8,128)(2,1)S(1)} all-to-all(bf16[64,25,576]{2,1,0:T(8,128)(2,1)S(1)} %copy.260), channel_id=1, replica_groups=mesh['wide'=8,'tensor'=4] {'wide'}, dimensions={0} | all-to-all | bytes 3686400 | tf_op jit(solution)/shard_map/all_to_all | solution.py:107
  1319.7 46.6 %reduce-scatter.47.cloned.1.call-done = f32[392,768]{1,0:T(8,128)} async-done(((f32[1568,768]{1,0:T(8,128)}), f32[392,768]{1,0:T(8,128)}) %reduce-scatter.47.cloned.1.call-update) | async-done | bytes 1204240 | tf_op jit(solution)/shard_map/reduce_scatter | solution.py:89
  1375.3 23.0 %all-gather.42.cloned.1.call-done = bf16[1568,768]{1,0:T(8,128)(2,1)} async-done(((bf16[392,768]{1,0:T(8,128)(2,1)}), bf16[1568,768]{1,0:T(8,128)(2,1)}) %all-gather.42.cloned.1.call-update) | async-done | bytes 2408464 | tf_op jit(solution)/shard_map/all_gather | solution.py:85
  1481.2 6.6 fusion.164
  1513.9 13.1 reduce-scatter.49.cloned.1.call-done
  1535.2 7.0 convolution_add_fusion
  1553.4 37.1 %all-reduce.6 = f32[3072]{0:T(1024)S(1)} all-reduce(f32[3072]{0:T(1024)S(1)} %add_dynamic-update-slice_fusion), channel_id=18, replica_groups=mesh['wide'=8,'tensor'=4] {'wide'}, use_global_device_ids=true, to_apply=%region_76.77.clone | all-reduce | flops 3072 | bytes 24576
  1595.2 68.3 %reduce-scatter.69.cloned.1.call-done = f32[96,576]{1,0:T(8,128)} async-done(((f32[768,576]{1,0:T(8,128)}), f32[96,576]{1,0:T(8,128)}) %reduce-scatter.69.cloned.1.call-update) | async-done | bytes 221200
  1665.4 63.4 %reduce-scatter.67.cloned.1.call-done = f32[96,192]{1,0:T(8,128)} async-done(((f32[768,192]{1,0:T(8,128)}), f32[96,192]{1,0:T(8,128)}) %reduce-scatter.67.cloned.1.call-update) | async-done | bytes 73744
  1730.4 68.4 %reduce-scatter.65.cloned.1.call-done = f32[96,576]{1,0:T(8,128)} async-done(((f32[768,576]{1,0:T(8,128)}), f32[96,576]{1,0:T(8,128)}) %reduce-scatter.65.cloned.1.call-update) | async-done | bytes 221200
  1804.9 58.3 %reduce-scatter.61.cloned.1.call-done = f32[96,3]{1,0:T(8,128)} async-done(((f32[768,3]{1,0:T(8,128)}), f32[96,3]{1,0:T(8,128)}) %reduce-scatter.61.cloned.1.call-update) | async-done | bytes 1168
  1864.0 63.5 %reduce-scatter.63.cloned.1.call-done = f32[96,10]{1,0:T(8,128)} async-done(((f32[768,10]{1,0:T(8,128)}), f32[96,10]{1,0:T(8,128)}) %reduce-scatter.63.cloned.1.call-update) | async-done | bytes 3856
  1928.4 10.7 all-reduce.7
  1939.1 61.1 %reduce-scatter.57.cloned.1.call-done = f32[96,768]{1,0:T(8,128)} async-done(((f32[768,768]{1,0:T(8,128)}), f32[96,768]{1,0:T(8,128)}) %reduce-scatter.57.cloned.1.call-update) | async-done | bytes 294928 | tf_op jit(solution)/shard_map/reduce_scatter | solution.py:117
  2000.2 73.1 %reduce-scatter.59.cloned.1.call-done = f32[768,96]{0,1:T(8,128)} async-done(((f32[768,768]{0,1:T(8,128)}), f32[768,96]{0,1:T(8,128)}) %reduce-scatter.59.cloned.1.call-update) | async-done | bytes 294928 | tf_op jit(solution)/shard_map/reduce_scatter | solution.py:118
  (666 shorter events, 455.5 us)
Async XLA Ops:
  8.0 58.0 %copy-start.6 = (bf16[2,392,768]{2,1,0:T(8,128)(2,1)S(1)}, bf16[2,392,768]{2,1,0:T(8,128)(2,1)}, u32[]{:S(2)}) copy-start(bf16[2,392,768]{2,1,0:T(8,128)(2,1)} %param.47) | copy-start | bytes 3612676
  8.0 130.5 %all-gather.30.cloned.1.call-start = ((), (), s32[]{:S(2)}) async-start(), calls=%async_computation.36 | async-start | bytes 3010560 | tf_op jit(solution)/shard_map/all_gather | solution.py:85
  66.0 203.7 %copy-start.101 = (f32[768]{0:T(1024)}, f32[768]{0:T(1024)S(1)}, u32[]{:S(2)}) copy-start(f32[768]{0:T(1024)S(1)} %get-tuple-element.308) | copy-start | bytes 9220
  67.6 76.5 %all-gather.20.cloned.1.call-start = ((), (), s32[]{:S(2)}) async-start(), calls=%async_computation.28 | async-start | bytes 3010560 | tf_op jit(solution)/shard_map/all_gather | solution.py:85
  68.3 146.2 %reduce-scatter.39.cloned.1.call-start = ((), (), s32[]{:S(2)}) async-start(), calls=%async_computation.37 | async-start | bytes 6021120 | tf_op jit(solution)/shard_map/reduce_scatter | solution.py:89
  167.1 98.5 %reduce-scatter.33.cloned.1.call-start = ((), (), s32[]{:S(2)}) async-start(), calls=%async_computation.29 | async-start | bytes 6021120 | tf_op jit(solution)/shard_map/reduce_scatter | solution.py:89
  184.9 126.6 %all-gather.22.cloned.1.call-start = ((), (), s32[]{:S(2)}) async-start(), calls=%async_computation.30 | async-start | bytes 3010560 | tf_op jit(solution)/shard_map/all_gather | solution.py:85
  267.7 380.7 %copy-start.8 = (f32[392,768]{1,0:T(8,128)}, f32[392,768]{1,0:T(8,128)S(1)}, u32[]{:S(2)}) copy-start(f32[392,768]{1,0:T(8,128)S(1)} %get-tuple-element.330) | copy-start | bytes 3612676
  271.2 50.3 %all-gather.32.cloned.1.call-start = ((), (), s32[]{:S(2)}) async-start(), calls=%async_computation.38 | async-start | bytes 3010560 | tf_op jit(solution)/shard_map/all_gather | solution.py:85
  413.8 50.1 %all-to-all-start.3 = ((bf16[64,25,192]{2,1,0:T(8,128)(2,1)}), bf16[64,25,192]{2,1,0:T(8,128)(2,1)S(1)}, u32[]{:S(2)}, u32[]{:S(2)}) async-start(bf16[64,25,192]{2,1,0:T(8,128)(2,1)} %copy.249), calls=%async_computation.7 | async-start | bytes 2097152 | tf_op jit(solution)/shard_map/all_to_all | solution.py:107
  417.4 184.8 %reduce-scatter.41.cloned.1.call-start = ((), (), s32[]{:S(2)}) async-start(), calls=%async_computation.39 | async-start | bytes 6021120 | tf_op jit(solution)/shard_map/reduce_scatter | solution.py:89
  471.5 176.8 %reduce-scatter.35.cloned.1.call-start = ((), (), s32[]{:S(2)}) async-start(), calls=%async_computation.31 | async-start | bytes 6021120 | tf_op jit(solution)/shard_map/reduce_scatter | solution.py:89
  601.5 46.8 %copy-start.11 = (f32[392,768]{1,0:T(8,128)S(1)}, f32[392,768]{1,0:T(8,128)}, u32[]{:S(2)}) copy-start(f32[392,768]{1,0:T(8,128)} %copy-done.10) | copy-start | bytes 3612676
  601.5 80.7 %all-gather.26.cloned.1.call-start = ((), (), s32[]{:S(2)}) async-start(), calls=%async_computation.33 | async-start | bytes 1327104 | tf_op jit(solution)/shard_map/all_gather | solution.py:150
  602.1 80.1 %all-gather.34.cloned.1.call-start = ((), (), s32[]{:S(2)}) async-start(), calls=%async_computation.40 | async-start | bytes 3010560 | tf_op jit(solution)/shard_map/all_gather | solution.py:85
  652.5 50.5 %all-gather.24.cloned.1.call-start = ((), (), s32[]{:S(2)}) async-start(), calls=%async_computation.32 | async-start | bytes 3010560 | tf_op jit(solution)/shard_map/all_gather | solution.py:85
  653.1 93.6 %all-gather.28.cloned.1.call-start = ((), (), s32[]{:S(2)}) async-start(), calls=%async_computation.34 | async-start | bytes 1327104 | tf_op jit(solution)/shard_map/all_gather | solution.py:151
  653.8 117.0 %all-gather.46.cloned.1.call-start = ((), (), s32[]{:S(2)}) async-start(), calls=%async_computation.55 | async-start | bytes 3010560 | tf_op jit(solution)/shard_map/all_gather | solution.py:85
  655.0 141.6 %all-gather.44.cloned.1.call-start = ((), (), s32[]{:S(2)}) async-start(), calls=%async_computation.54 | async-start | bytes 3010560 | tf_op jit(solution)/shard_map/all_gather | solution.py:85
  655.7 191.8 %reduce-scatter.51.cloned.1.call-start = ((), (), s32[]{:S(2)}) async-start(), calls=%async_computation.47 | async-start | bytes 6021120 | tf_op jit(solution)/shard_map/reduce_scatter | solution.py:89
  785.5 113.0 %reduce-scatter.45.cloned.1.call-start = ((), (), s32[]{:S(2)}) async-start(), calls=%async_computation.42 | async-start | bytes 6021120 | tf_op jit(solution)/shard_map/reduce_scatter | solution.py:89
  810.6 138.8 %reduce-scatter.37.cloned.1.call-start = ((), (), s32[]{:S(2)}) async-start(), calls=%async_computation.35 | async-start | bytes 6021120 | tf_op jit(solution)/shard_map/reduce_scatter | solution.py:89
  816.6 183.9 %reduce-scatter.43.cloned.1.call-start = ((), (), s32[]{:S(2)}) async-start(), calls=%async_computation.41 | async-start | bytes 6021120 | tf_op jit(solution)/shard_map/reduce_scatter | solution.py:89
  822.7 75.8 %copy-start.14 = (f32[392,768]{1,0:T(8,128)S(1)}, f32[392,768]{1,0:T(8,128)}, u32[]{:S(2)}) copy-start(f32[392,768]{1,0:T(8,128)} %copy-done.13) | copy-start | bytes 3612676
  822.7 75.8 %copy-start.16 = (f32[392,768]{1,0:T(8,128)S(1)}, f32[392,768]{1,0:T(8,128)}, u32[]{:S(2)}) copy-start(f32[392,768]{1,0:T(8,128)} %copy-done.15) | copy-start | bytes 3612676
  822.7 177.8 %copy-start.125 = (f32[768]{0:T(1024)S(1)}, f32[768]{0:T(1024)}, u32[]{:S(2)}) copy-start(f32[768]{0:T(1024)} %get-tuple-element.301) | copy-start | bytes 9220
  822.7 208.8 %all-gather.40.cloned.1.call-start = ((), (), s32[]{:S(2)}) async-start(), calls=%async_computation.48 | async-start | bytes 3010560 | tf_op jit(solution)/shard_map/all_gather | solution.py:85
  1099.5 62.3 %all-to-all-start.7 = ((bf16[64,25,576]{2,1,0:T(8,128)(2,1)}), bf16[64,25,576]{2,1,0:T(8,128)(2,1)S(1)}, u32[]{:S(2)}, u32[]{:S(2)}) async-start(bf16[64,25,576]{2,1,0:T(8,128)(2,1)} %copy.282), calls=%async_computation.17 | async-start | bytes 5242880 | tf_op jit(solution)/shard_map/all_to_all | solution.py:107
  1103.1 76.3 %all-gather.36.cloned.1.call-start = ((), (), s32[]{:S(2)}) async-start(), calls=%async_computation.43 | async-start | bytes 3010560 | tf_op jit(solution)/shard_map/all_gather | solution.py:85
  1103.7 216.0 %reduce-scatter.53.cloned.1.call-start = ((), (), s32[]{:S(2)}) async-start(), calls=%async_computation.49 | async-start | bytes 6021120 | tf_op jit(solution)/shard_map/reduce_scatter | solution.py:89
  1179.3 187.0 %reduce-scatter.47.cloned.1.call-start = ((), (), s32[]{:S(2)}) async-start(), calls=%async_computation.44 | async-start | bytes 6021120 | tf_op jit(solution)/shard_map/reduce_scatter | solution.py:89
  1319.6 46.8 %copy-start.104 = (f32[392]{0:T(512)S(1)}, f32[392]{0:T(512)}, u32[]{:S(2)}) copy-start(f32[392]{0:T(512)} %copy-done.103) | copy-start | bytes 4708
  1319.6 46.8 %copy-start.106 = (f32[392]{0:T(512)S(1)}, f32[392]{0:T(512)}, u32[]{:S(2)}) copy-start(f32[392]{0:T(512)} %copy-done.105) | copy-start | bytes 4708
  1319.6 49.5 %copy-start.122 = (f32[392]{0:T(512)S(1)}, f32[392]{0:T(512)}, u32[]{:S(2)}) copy-start(f32[392]{0:T(512)} %copy-done.121) | copy-start | bytes 4708
  1319.6 49.5 %copy-start.124 = (f32[392]{0:T(512)S(1)}, f32[392]{0:T(512)}, u32[]{:S(2)}) copy-start(f32[392]{0:T(512)} %copy-done.123) | copy-start | bytes 4708
  1319.7 78.6 %all-gather.42.cloned.1.call-start = ((), (), s32[]{:S(2)}) async-start(), calls=%async_computation.50 | async-start | bytes 3010560 | tf_op jit(solution)/shard_map/all_gather | solution.py:85
  1373.8 53.4 %all-gather.38.cloned.1.call-start = ((), (), s32[]{:S(2)}) async-start(), calls=%async_computation.45 | async-start | bytes 3010560 | tf_op jit(solution)/shard_map/all_gather | solution.py:85
  1374.8 139.1 %reduce-scatter.55.cloned.1.call-start = ((), (), s32[]{:S(2)}) async-start(), calls=%async_computation.51 | async-start | bytes 6021120 | tf_op jit(solution)/shard_map/reduce_scatter | solution.py:89
  1426.8 100.2 %reduce-scatter.49.cloned.1.call-start = ((), (), s32[]{:S(2)}) async-start(), calls=%async_computation.46 | async-start | bytes 6021120 | tf_op jit(solution)/shard_map/reduce_scatter | solution.py:89
  1457.6 135.9 %reduce-scatter.71.cloned.1.call-start = ((), (), s32[]{:S(2)}) async-start(), calls=%async_computation.61 | async-start | bytes 884736
  1464.2 199.3 %reduce-scatter.69.cloned.1.call-start = ((), (), s32[]{:S(2)}) async-start(), calls=%async_computation.60 | async-start | bytes 2211840
  1480.5 248.3 %reduce-scatter.67.cloned.1.call-start = ((), (), s32[]{:S(2)}) async-start(), calls=%async_computation.59 | async-start | bytes 884736
  1497.4 301.4 %reduce-scatter.65.cloned.1.call-start = ((), (), s32[]{:S(2)}) async-start(), calls=%async_computation.58 | async-start | bytes 2211840
  1513.5 349.7 %reduce-scatter.61.cloned.1.call-start = ((), (), s32[]{:S(2)}) async-start(), calls=%async_computation.56 | async-start | bytes 442368
  1533.9 393.7 %reduce-scatter.63.cloned.1.call-start = ((), (), s32[]{:S(2)}) async-start(), calls=%async_computation.57 | async-start | bytes 442368
  1535.2 465.0 %reduce-scatter.57.cloned.1.call-start = ((), (), s32[]{:S(2)}) async-start(), calls=%async_computation.52 | async-start | bytes 2654208 | tf_op jit(solution)/shard_map/reduce_scatter | solution.py:117
  1542.3 531.0 %reduce-scatter.59.cloned.1.call-start = ((), (), s32[]{:S(2)}) async-start(), calls=%async_computation.53 | async-start | bytes 2654208 | tf_op jit(solution)/shard_map/reduce_scatter | solution.py:118
  1590.6 210.1 %copy-start.25 = (f32[392,768]{1,0:T(8,128)S(1)}, f32[392,768]{1,0:T(8,128)}, u32[]{:S(2)}) copy-start(f32[392,768]{1,0:T(8,128)} %copy-done.24) | copy-start | bytes 3612676
  (130 other events, 1100.1 us)
Sparse Core Ops, SparseCore 0:
  67.7 21.6 all-gather.29
  91.5 24.3 all-gather.19
  167.2 47.2 reduce-scatter.38
  217.0 48.5 reduce-scatter.32
  271.3 24.3 all-gather.21
  297.1 24.3 all-gather.31
  471.6 46.6 reduce-scatter.40
  601.6 46.6 reduce-scatter.34
  1007.1 24.3 all-gather.39
  1105.2 24.7 all-gather.35
  1373.9 24.3 all-gather.41
  1399.7 24.3 all-gather.37
  1426.9 48.9 reduce-scatter.54
  1478.4 48.5 reduce-scatter.48
  1530.1 63.3 reduce-scatter.70
  1596.9 66.5 reduce-scatter.68
  1666.6 62.1 reduce-scatter.66
  1732.1 66.6 reduce-scatter.64
  1802.1 61.0 reduce-scatter.60
  1866.3 61.2 reduce-scatter.62
  1931.6 68.5 reduce-scatter.56
  2004.3 68.9 reduce-scatter.58
Sparse Core Ops, SparseCore 1:
  604.2 39.5 all-gather.25
  652.6 24.2 all-gather.33
  678.8 24.2 all-gather.23
  705.2 41.4 all-gather.27
  748.3 22.5 all-gather.45
  772.4 24.2 all-gather.43
  799.1 48.4 reduce-scatter.50
  850.0 48.4 reduce-scatter.44
  900.9 48.4 reduce-scatter.36
  952.0 48.4 reduce-scatter.42
  1179.4 46.6 reduce-scatter.52
  1319.7 46.5 reduce-scatter.46
where the time goes:
time: 2090 us; the launch traced here: 2080 us
  waiting for transfers between devices  1000 us (48%)
  blocking collectives  520 us (25%)
  local copies, waits for them, and re-layouts  244 us (12%)
  matrix products  216 us (10%)
  other arithmetic  68.4 us (3%)
    reduce_scatter x12, waiting for transfers between devices, sum_rows(): lax.psum_scatter(term(jnp.int32(0), row_count * lax.axis_size('tensor')),...  362 us
    unnamed x40, waiting for transfers between devices  327 us
    all_to_all x4, blocking collectives, to_patches(): lax.all_to_all(padded, 'wide', split_axis=1, concat_axis=0, tiled=True)  153 us
    all_gather x12, waiting for transfers between devices, gather_rows(): return lax.all_gather(block, 'tensor', axis=0, tiled=True)  101 us
    all_to_all x2, blocking collectives, to_frames(): lax.all_to_all(block, 'wide', split_axis=0, concat_axis=1, tiled=True)  89.5 us
    reduce_scatter x1, waiting for transfers between devices, reduce_wide(): lax.psum_scatter(packed[5], 'wide', scatter_dimension=1, tiled=True)  73.1 us
    unnamed x313, local copies, waits for them, and re-layouts  63.9 us
    reduce_scatter x1, waiting for transfers between devices, reduce_wide(): lax.psum_scatter(packed[4], 'wide', scatter_dimension=0, tiled=True)  61.1 us
  transfers between devices with their start and end apart: 36, of which 25 were waited for; matrix products, arithmetic and copies ran while one was open for 18% of the time, Pallas kernels for 0%

commit v1 on v0

--- a/solution.py
+++ b/solution.py
@@ -8,6 +8,19 @@
 FRAMES = 16
 FRAME_RUN = 2
 EPSILON = 1e-06
+
+
+def collect(shard, axis, dim):
+    ways = lax.axis_size(axis)
+    up = [(d, (d + 1) % ways) for d in range(ways)]
+    down = [(d, (d - 1) % ways) for d in range(ways)]
+    earlier, later = ([shard], [shard])
+    for _ in range(ways // 2):
+        earlier.append(lax.ppermute(earlier[-1], axis, up))
+    for _ in range((ways - 1) // 2):
+        later.append(lax.ppermute(later[-1], axis, down))
+    line = jnp.concatenate([*earlier[::-1], *later[1:]], axis=dim)
+    return jnp.roll(line, (lax.axis_index(axis) - ways // 2) * shard.shape[dim], axis=dim)
 
 
 def layer_norm(rows, gain, shift):
@@ -82,7 +95,7 @@
 
 
 def gather_rows(block):
-    return lax.all_gather(block, "tensor", axis=0, tiled=True)
+    return collect(block, "tensor", 0)
 
 
 def sum_rows(term, row_count):

time: 2090 us -> 2230 us (1.067)
  other arithmetic: 68.4 us -> 240 us
  waiting for transfers between devices: 1000 us -> 960 us
  starting transfers between devices: 11.1 us -> 36.6 us
    concatenate x0 -> x12, other arithmetic: none -> 164 us  [collect(): jnp.roll(line, (lax.axis_index(axis) - ways // 2) * shard.shape[dim], axi...]
    ppermute x0 -> x36, waiting for transfers between devices: none -> 131 us  [the longest x24 117 us: collect(): earlier.append(lax.ppermute(earlier[-1], axis, up))]
    all_gather x12 -> x0, waiting for transfers between devices: 101 us -> none  [gather_rows(): return lax.all_gather(block, 'tensor', axis=0, tiled=True)]
    reduce_scatter x12, waiting for transfers between devices: 362 us -> 321 us  [sum_rows(): lax.psum_scatter(term(jnp.int32(0), row_count * lax.axis_size('tensor')),...]
    ppermute x0 -> x36, starting transfers between devices: none -> 28.1 us  [the longest x12 14.1 us: collect(): later.append(lax.ppermute(later[-1], axis, down))]
    dot_general x2, matrix products: 31 us -> 6.39 us  [per_device(): jnp.dot(full_m, fetched[4], preferred_element_type=jnp.float32) + up_bias]
    unnamed x40 -> x28, waiting for transfers between devices: 327 us -> 317 us
    unnamed x313 -> x343, local copies, waits for them, and re-layouts: 63.9 us -> 70.4 us
  transfers between devices with their start and end apart: 36 -> 60, of which waited for: 25 -> 31; matrix products, arithmetic and copies ran while one was open for 18% -> 18% of each run, Pallas kernels for 0% -> 0%
where the time goes in v1:
time: 2230 us; the launch traced here: 2220 us
  waiting for transfers between devices  960 us (43%)
  blocking collectives  518 us (23%)
  local copies, waits for them, and re-layouts  254 us (11%)
  other arithmetic  240 us (11%)
  matrix products  195 us (9%)
  starting transfers between devices  36.6 us (2%)
    reduce_scatter x12, waiting for transfers between devices, sum_rows(): lax.psum_scatter(term(jnp.int32(0), row_count * lax.axis_size('tensor')),...  321 us
    unnamed x28, waiting for transfers between devices  317 us
    concatenate x12, other arithmetic, collect(): jnp.roll(line, (lax.axis_index(axis) - ways // 2) * shard.shape[dim], axi...  164 us
    all_to_all x4, blocking collectives, to_patches(): lax.all_to_all(padded, 'wide', split_axis=1, concat_axis=0, tiled=True)  145 us
    ppermute x24, waiting for transfers between devices, collect(): earlier.append(lax.ppermute(earlier[-1], axis, up))  117 us
    all_to_all x2, blocking collectives, to_frames(): lax.all_to_all(block, 'wide', split_axis=0, concat_axis=1, tiled=True)  89.6 us
    reduce_scatter x1, waiting for transfers between devices, reduce_wide(): lax.psum_scatter(packed[4], 'wide', scatter_dimension=0, tiled=True)  72.9 us
    unnamed x343, local copies, waits for them, and re-layouts  70.4 us
  transfers between devices with their start and end apart: 60, of which 31 were waited for; matrix products, arithmetic and copies ran while one was open for 18% of the time, Pallas kernels for 0%

profile of v1, /device:TPU:0, one launch (start us, length us, event | category | flops | bytes accessed | tf_op | source)
XLA Modules:
  0.0 2223.4 jit_solution(7892107254683914165)
XLA Ops:
  11.5 22.3 %all-gather = bf16[8,96,3]{1,2,0:T(4,128)(2,1)S(1)} all-gather(bf16[1,96,3]{1,2,0:T(4,128)(2,1)S(1)} %bitcast.565), channel_id=1, replica_groups=mesh['wide'=8,'tensor'=4] {'wide'}, dimensions={0}, use_global_device_ids=true | all-gather | bytes 5184 | tf_op jit(solution)/shard_map/all_gather | solution.py:165
  34.0 30.6 %all-gather.1 = bf16[8,96,10]{1,2,0:T(8,128)(2,1)S(1)} all-gather(bf16[1,96,10]{1,2,0:T(8,128)(2,1)S(1)} %bitcast.562), channel_id=1, replica_groups=mesh['wide'=8,'tensor'=4] {'wide'}, dimensions={0}, use_global_device_ids=true | all-gather | bytes 17280 | tf_op jit(solution)/shard_map/all_gather | solution.py:166
  69.5 10.6 collective-permute-done.9
  80.1 40.6 %all_gather.20 = bf16[3,768,192]{2,0,1:T(4,128)(2,1)} all-gather(bf16[3,96,192]{2,0,1:T(4,128)(2,1)S(1)} %copy.214), channel_id=1, replica_groups=mesh['wide'=8,'tensor'=4] {'wide'}, dimensions={1}, use_global_device_ids=true | all-gather | bytes 995328 | tf_op jit(solution)/shard_map/all_gather | solution.py:159
  124.5 31.0 %all_gather.21 = bf16[192,768]{0,1:T(8,128)(2,1)S(1)} all-gather(bf16[192,96]{0,1:T(8,128)(2,1)S(1)} %copy.221), channel_id=1, replica_groups=mesh['wide'=8,'tensor'=4] {'wide'}, dimensions={1}, use_global_device_ids=true | all-gather | bytes 331776 | tf_op jit(solution)/shard_map/all_gather | solution.py:160
  155.6 11.8 fusion.73
  169.2 14.0 fusion.94
  221.8 29.8 %reduce-scatter.39.cloned.1.call-done = f32[392,768]{1,0:T(8,128)} async-done(((f32[1568,768]{1,0:T(8,128)}), f32[392,768]{1,0:T(8,128)}) %reduce-scatter.39.cloned.1.call-update) | async-done | bytes 1204240 | tf_op jit(solution)/shard_map/reduce_scatter | solution.py:102
  251.7 51.2 %reduce-scatter.33.cloned.1.call-done = f32[392,768]{1,0:T(8,128)} async-done(((f32[1568,768]{1,0:T(8,128)}), f32[392,768]{1,0:T(8,128)}) %reduce-scatter.33.cloned.1.call-update) | async-done | bytes 1204240 | tf_op jit(solution)/shard_map/reduce_scatter | solution.py:102
  309.5 13.7 collective-permute-done.12
  323.3 37.6 %all_gather.22 = bf16[3,768,192]{2,0,1:T(4,128)(2,1)S(1)} all-gather(bf16[3,96,192]{2,0,1:T(4,128)(2,1)S(1)} %copy.222), channel_id=1, replica_groups=mesh['wide'=8,'tensor'=4] {'wide'}, dimensions={1}, use_global_device_ids=true | all-gather | bytes 995328 | tf_op jit(solution)/shard_map/all_gather | solution.py:161
  377.2 16.3 fusion.87
  408.7 50.6 %all_to_all.132 = bf16[8,200,576]{2,0,1:T(8,128)(2,1)S(1)} all-to-all(bf16[8,200,576]{2,0,1:T(8,128)(2,1)S(1)} %pad.52.clone), channel_id=1, replica_groups=mesh['wide'=8,'tensor'=4] {'wide'}, dimensions={1} | all-to-all | bytes 3686400 | tf_op jit(solution)/shard_map/all_to_all | solution.py:116
  485.3 46.1 %all_gather.23 = bf16[192,768]{0,1:T(8,128)(2,1)S(1)} all-gather(bf16[192,96]{0,1:T(8,128)(2,1)S(1)} %copy.234), channel_id=1, replica_groups=mesh['wide'=8,'tensor'=4] {'wide'}, dimensions={1}, use_global_device_ids=true | all-gather | bytes 331776 | tf_op jit(solution)/shard_map/all_gather | solution.py:162
  552.6 45.4 %all_to_all.133 = bf16[8,200,576]{2,0,1:T(8,128)(2,1)} all-to-all(bf16[8,200,576]{2,0,1:T(8,128)(2,1)S(1)} %pad.53.clone), channel_id=1, replica_groups=mesh['wide'=8,'tensor'=4] {'wide'}, dimensions={1} | all-to-all | bytes 3686400 | tf_op jit(solution)/shard_map/all_to_all | solution.py:116
  631.6 27.4 %all_to_all.134 = bf16[64,25,192]{2,1,0:T(8,128)(2,1)S(1)} all-to-all(bf16[64,25,192]{2,1,0:T(8,128)(2,1)S(1)} %copy.249), channel_id=1, replica_groups=mesh['wide'=8,'tensor'=4] {'wide'}, dimensions={0} | all-to-all | bytes 1228800 | tf_op jit(solution)/shard_map/all_to_all | solution.py:120
  674.8 26.2 %all-gather.2 = bf16[8,1,384]{2,1,0:T(2,128)(2,1)S(1)} all-gather(bf16[1,1,384]{2,1,0:T(2,128)(2,1)S(1)} %reshape.848), channel_id=1, replica_groups=mesh['wide'=8,'tensor'=4] {'wide'}, dimensions={0}, use_global_device_ids=true | all-gather | bytes 6912 | tf_op jit(solution)/shard_map/all_gather | solution.py:167
  712.7 24.7 %reduce-scatter.41.cloned.1.call-done = f32[392,768]{1,0:T(8,128)} async-done(((f32[1568,768]{1,0:T(8,128)}), f32[392,768]{1,0:T(8,128)}) %reduce-scatter.41.cloned.1.call-update) | async-done | bytes 1204240 | tf_op jit(solution)/shard_map/reduce_scatter | solution.py:102
  787.6 15.3 fusion.59
  811.1 27.1 %convert_reduce_fusion.1 = (f32[768]{0:T(1024)}, bf16[1568,768]{1,0:T(8,128)(2,1)S(1)}, f32[1568,768]{1,0:T(8,128)}, f32[768]{0:T(1024)}, bf16[1568,768]{1,0:T(8,128)(2,1)}, /*index=5*/f32[1568,768]{1,0:T(8,128)}) fusion(f32[1568,768]{1,0:T(8,128)S(1)} %fusion.219, f32[768]{0:T(1024)S(1)} %dynamic_slice.27, f32[1568,768]{1,0:T(8,128)S(1)} %bitcast.567, ...), kind=kOutput, calls=%fused_computation.111 | convolution fusion | flops 2030320128 | bytes 32498688 | tf_op jit(solution)/shard_map/gd,fd->gf/dot_general | solution.py:254
  851.5 10.9 multiply_convert_fusion.3
  876.0 16.8 reduce-scatter.45.cloned.1.call-done
  892.8 51.0 %reduce-scatter.51.cloned.1.call-done = f32[392,768]{1,0:T(8,128)} async-done(((f32[1568,768]{1,0:T(8,128)}), f32[392,768]{1,0:T(8,128)}) %reduce-scatter.51.cloned.1.call-update) | async-done | bytes 1204240 | tf_op jit(solution)/shard_map/reduce_scatter | solution.py:102
  947.1 47.9 %reduce-scatter.37.cloned.1.call-done = f32[392,768]{1,0:T(8,128)} async-done(((f32[1568,768]{1,0:T(8,128)}), f32[392,768]{1,0:T(8,128)}) %reduce-scatter.37.cloned.1.call-update) | async-done | bytes 1204240 | tf_op jit(solution)/shard_map/reduce_scatter | solution.py:102
  995.0 51.2 %reduce-scatter.43.cloned.1.call-done = f32[392,768]{1,0:T(8,128)} async-done(((f32[1568,768]{1,0:T(8,128)}), f32[392,768]{1,0:T(8,128)}) %reduce-scatter.43.cloned.1.call-update) | async-done | bytes 1204240 | tf_op jit(solution)/shard_map/reduce_scatter | solution.py:102
  1054.2 13.5 collective-permute-done.21
  1077.4 17.6 fusion.45
  1099.9 24.6 %all_to_all.135 = bf16[8,200,192]{2,0,1:T(8,128)(2,1)S(1)} all-to-all(bf16[8,200,192]{2,0,1:T(8,128)(2,1)S(1)} %pad.54), channel_id=1, replica_groups=mesh['wide'=8,'tensor'=4] {'wide'}, dimensions={1} | all-to-all | bytes 1228800 | tf_op jit(solution)/shard_map/all_to_all | solution.py:116
  1163.0 57.3 %all-to-all-done.5 = bf16[64,25,576]{2,1,0:T(8,128)(2,1)S(1)} async-done(((bf16[64,25,576]{2,1,0:T(8,128)(2,1)}), bf16[64,25,576]{2,1,0:T(8,128)(2,1)S(1)}, u32[]{:S(2)}, u32[]{:S(2)}) %all-to-all-start.5) | async-done | bytes 1843232 | tf_op jit(solution)/shard_map/all_to_all | solution.py:120
  1239.9 11.9 collective-permute-done.32
  1256.7 16.3 fusion.24
  1278.0 24.8 %all_to_all.136 = bf16[8,200,192]{2,0,1:T(8,128)(2,1)S(1)} all-to-all(bf16[8,200,192]{2,0,1:T(8,128)(2,1)S(1)} %pad.55), channel_id=1, replica_groups=mesh['wide'=8,'tensor'=4] {'wide'}, dimensions={1} | all-to-all | bytes 1228800 | tf_op jit(solution)/shard_map/all_to_all | solution.py:116
  1332.9 62.2 %all_to_all.137 = bf16[64,25,576]{2,1,0:T(8,128)(2,1)S(1)} all-to-all(bf16[64,25,576]{2,1,0:T(8,128)(2,1)S(1)} %copy.282), channel_id=1, replica_groups=mesh['wide'=8,'tensor'=4] {'wide'}, dimensions={0} | all-to-all | bytes 3686400 | tf_op jit(solution)/shard_map/all_to_all | solution.py:120
  1412.6 48.7 %reduce-scatter.53.cloned.1.call-done = f32[392,768]{1,0:T(8,128)} async-done(((f32[1568,768]{1,0:T(8,128)}), f32[392,768]{1,0:T(8,128)}) %reduce-scatter.53.cloned.1.call-update) | async-done | bytes 1204240 | tf_op jit(solution)/shard_map/reduce_scatter | solution.py:102
  1469.7 13.5 collective-permute-done.33
  1492.8 17.8 fusion.17
  1543.6 13.5 collective-permute-done.24
  1557.1 16.6 collective-permute-done.25
  1573.7 17.8 fusion.38
  1702.2 37.9 %all-reduce.6 = f32[3072]{0:T(1024)S(1)} all-reduce(f32[3072]{0:T(1024)S(1)} %add_dynamic-update-slice_fusion), channel_id=16, replica_groups=mesh['wide'=8,'tensor'=4] {'wide'}, use_global_device_ids=true, to_apply=%region_76.78.clone | all-reduce | flops 3072 | bytes 24576
  1744.1 62.4 %reduce-scatter.69.cloned.1.call-done = f32[96,576]{1,0:T(8,128)} async-done(((f32[768,576]{1,0:T(8,128)}), f32[96,576]{1,0:T(8,128)}) %reduce-scatter.69.cloned.1.call-update) | async-done | bytes 221200
  1808.3 63.4 %reduce-scatter.67.cloned.1.call-done = f32[96,192]{1,0:T(8,128)} async-done(((f32[768,192]{1,0:T(8,128)}), f32[96,192]{1,0:T(8,128)}) %reduce-scatter.67.cloned.1.call-update) | async-done | bytes 73744
  1873.4 68.1 %reduce-scatter.65.cloned.1.call-done = f32[96,576]{1,0:T(8,128)} async-done(((f32[768,576]{1,0:T(8,128)}), f32[96,576]{1,0:T(8,128)}) %reduce-scatter.65.cloned.1.call-update) | async-done | bytes 221200
  1947.6 58.3 %reduce-scatter.61.cloned.1.call-done = f32[96,3]{1,0:T(8,128)} async-done(((f32[768,3]{1,0:T(8,128)}), f32[96,3]{1,0:T(8,128)}) %reduce-scatter.61.cloned.1.call-update) | async-done | bytes 1168
  2006.8 63.4 %reduce-scatter.63.cloned.1.call-done = f32[96,10]{1,0:T(8,128)} async-done(((f32[768,10]{1,0:T(8,128)}), f32[96,10]{1,0:T(8,128)}) %reduce-scatter.63.cloned.1.call-update) | async-done | bytes 3856
  2071.1 10.7 all-reduce.7
  2081.8 61.2 %reduce-scatter.59.cloned.1.call-done = f32[768,96]{0,1:T(8,128)} async-done(((f32[768,768]{0,1:T(8,128)}), f32[768,96]{0,1:T(8,128)}) %reduce-scatter.59.cloned.1.call-update) | async-done | bytes 294928 | tf_op jit(solution)/shard_map/reduce_scatter | solution.py:131
  2142.9 72.9 %reduce-scatter.57.cloned.1.call-done = f32[96,768]{1,0:T(8,128)} async-done(((f32[768,768]{1,0:T(8,128)}), f32[96,768]{1,0:T(8,128)}) %reduce-scatter.57.cloned.1.call-update) | async-done | bytes 294928 | tf_op jit(solution)/shard_map/reduce_scatter | solution.py:130
  (745 shorter events, 599.4 us)
Async XLA Ops:
  8.1 243.6 %reduce-scatter.39.cloned.1.call-start = ((), (), s32[]{:S(2)}) async-start(), calls=%async_computation.33 | async-start | bytes 6021120 | tf_op jit(solution)/shard_map/reduce_scatter | solution.py:102
  65.9 103.3 %collective-permute-start.2 = (bf16[392,768]{1,0:T(8,128)(2,1)S(1)}, bf16[392,768]{1,0:T(8,128)(2,1)}, u32[]{:S(2)}, u32[]{:S(2)}) collective-permute-start(bf16[392,768]{1,0:T(8,128)(2,1)S(1)} %get-tuple-element.354), channel_id=1, source_target_pairs={{0,3},{1,0},{2,1},{3,2},{4,7},{5,4},{6,5},{7,6},{8,11},{9,8},{10,9... | collective-permute-start | bytes 1806344 | tf_op jit(solution)/shard_map/ppermute | solution.py:21
  67.6 87.9 %collective-permute-start = (bf16[392,768]{1,0:T(8,128)(2,1)S(1)}, bf16[392,768]{1,0:T(8,128)(2,1)}, u32[]{:S(2)}, u32[]{:S(2)}) collective-permute-start(bf16[392,768]{1,0:T(8,128)(2,1)S(1)} %get-tuple-element.354), channel_id=1, source_target_pairs={{0,1},{1,2},{2,3},{3,0},{4,5},{5,6},{6,7},{7,4},{8,9},{9,10},{10,1... | collective-permute-start | bytes 1806344 | tf_op jit(solution)/shard_map/ppermute | solution.py:19
  67.6 88.0 %collective-permute-start.11 = (bf16[392,768]{1,0:T(8,128)(2,1)S(1)}, bf16[392,768]{1,0:T(8,128)(2,1)}, u32[]{:S(2)}, u32[]{:S(2)}) collective-permute-start(bf16[392,768]{1,0:T(8,128)(2,1)S(1)} %get-tuple-element.355), channel_id=1, source_target_pairs={{0,3},{1,0},{2,1},{3,2},{4,7},{5,4},{6,5},{7,6},{8,11},{9,8},{10,9... | collective-permute-start | bytes 1806344 | tf_op jit(solution)/shard_map/ppermute | solution.py:21
  80.1 75.5 %collective-permute-start.10 = (bf16[392,768]{1,0:T(8,128)(2,1)}, bf16[392,768]{1,0:T(8,128)(2,1)}, u32[]{:S(2)}, u32[]{:S(2)}) collective-permute-start(bf16[392,768]{1,0:T(8,128)(2,1)} %collective-permute-done.9), channel_id=1, source_target_pairs={{0,1},{1,2},{2,3},{3,0},{4,5},{5,6},{6,7},{7,4},{8,9},{9,10},{10,1... | collective-permute-start | bytes 1806344 | tf_op jit(solution)/shard_map/ppermute | solution.py:19
  204.4 98.4 %reduce-scatter.33.cloned.1.call-start = ((), (), s32[]{:S(2)}) async-start(), calls=%async_computation.28 | async-start | bytes 6021120 | tf_op jit(solution)/shard_map/reduce_scatter | solution.py:102
  307.6 15.5 collective-permute-start.12
  307.7 55.3 %collective-permute-start.3 = (bf16[392,768]{1,0:T(8,128)(2,1)S(1)}, bf16[392,768]{1,0:T(8,128)(2,1)}, u32[]{:S(2)}, u32[]{:S(2)}) collective-permute-start(bf16[392,768]{1,0:T(8,128)(2,1)S(1)} %get-tuple-element.377), channel_id=1, source_target_pairs={{0,1},{1,2},{2,3},{3,0},{4,5},{5,6},{6,7},{7,4},{8,9},{9,10},{10,1... | collective-permute-start | bytes 1806344 | tf_op jit(solution)/shard_map/ppermute | solution.py:19
  308.2 55.3 %collective-permute-start.14 = (bf16[392,768]{1,0:T(8,128)(2,1)}, bf16[392,768]{1,0:T(8,128)(2,1)}, u32[]{:S(2)}, u32[]{:S(2)}) collective-permute-start(bf16[392,768]{1,0:T(8,128)(2,1)} %get-tuple-element.378), channel_id=1, source_target_pairs={{0,3},{1,0},{2,1},{3,2},{4,7},{5,4},{6,5},{7,6},{8,11},{9,8},{10,9... | collective-permute-start | bytes 1806344 | tf_op jit(solution)/shard_map/ppermute | solution.py:21
  323.2 40.3 %collective-permute-start.13 = (bf16[392,768]{1,0:T(8,128)(2,1)}, bf16[392,768]{1,0:T(8,128)(2,1)}, u32[]{:S(2)}, u32[]{:S(2)}) collective-permute-start(bf16[392,768]{1,0:T(8,128)(2,1)} %collective-permute-done.12), channel_id=1, source_target_pairs={{0,1},{1,2},{2,3},{3,0},{4,5},{5,6},{6,7},{7,4},{8,9},{9,10},{10,1... | collective-permute-start | bytes 1806344 | tf_op jit(solution)/shard_map/ppermute | solution.py:19
  481.6 49.9 %all-to-all-start.1 = ((bf16[64,25,192]{2,1,0:T(8,128)(2,1)}), bf16[64,25,192]{2,1,0:T(8,128)(2,1)S(1)}, u32[]{:S(2)}, u32[]{:S(2)}) async-start(bf16[64,25,192]{2,1,0:T(8,128)(2,1)} %copy.231), calls=%async_computation.2 | async-start | bytes 2097152 | tf_op jit(solution)/shard_map/all_to_all | solution.py:120
  485.2 227.5 %reduce-scatter.35.cloned.1.call-start = ((), (), s32[]{:S(2)}) async-start(), calls=%async_computation.29 | async-start | bytes 6021120 | tf_op jit(solution)/shard_map/reduce_scatter | solution.py:102
  539.0 198.3 %reduce-scatter.41.cloned.1.call-start = ((), (), s32[]{:S(2)}) async-start(), calls=%async_computation.34 | async-start | bytes 6021120 | tf_op jit(solution)/shard_map/reduce_scatter | solution.py:102
  668.5 94.0 %all-gather.8.cloned.1.call-start = ((), (), s32[]{:S(2)}) async-start(), calls=%async_computation.31 | async-start | bytes 1327104 | tf_op jit(solution)/shard_map/all_gather | solution.py:164
  669.1 133.8 %all-gather.6.cloned.1.call-start = ((), (), s32[]{:S(2)}) async-start(), calls=%async_computation.30 | async-start | bytes 1327104 | tf_op jit(solution)/shard_map/all_gather | solution.py:163
  671.5 29.6 %collective-permute-start.18 = (bf16[392,768]{1,0:T(8,128)(2,1)}, bf16[392,768]{1,0:T(8,128)(2,1)}, u32[]{:S(2)}, u32[]{:S(2)}) collective-permute-start(bf16[392,768]{1,0:T(8,128)(2,1)} %get-tuple-element.364), channel_id=1, source_target_pairs={{0,1},{1,2},{2,3},{3,0},{4,5},{5,6},{6,7},{7,4},{8,9},{9,10},{10,1... | collective-permute-start | bytes 1806344 | tf_op jit(solution)/shard_map/ppermute | solution.py:19
  671.5 32.6 %collective-permute-start.27 = (bf16[392,768]{1,0:T(8,128)(2,1)}, bf16[392,768]{1,0:T(8,128)(2,1)}, u32[]{:S(2)}, u32[]{:S(2)}) collective-permute-start(bf16[392,768]{1,0:T(8,128)(2,1)} %get-tuple-element.365), channel_id=1, source_target_pairs={{0,1},{1,2},{2,3},{3,0},{4,5},{5,6},{6,7},{7,4},{8,9},{9,10},{10,1... | collective-permute-start | bytes 1806344 | tf_op jit(solution)/shard_map/ppermute | solution.py:19
  674.6 67.0 %collective-permute-start.20 = (bf16[392,768]{1,0:T(8,128)(2,1)}, bf16[392,768]{1,0:T(8,128)(2,1)}, u32[]{:S(2)}, u32[]{:S(2)}) collective-permute-start(bf16[392,768]{1,0:T(8,128)(2,1)} %get-tuple-element.364), channel_id=1, source_target_pairs={{0,3},{1,0},{2,1},{3,2},{4,7},{5,4},{6,5},{7,6},{8,11},{9,8},{10,9... | collective-permute-start | bytes 1806344 | tf_op jit(solution)/shard_map/ppermute | solution.py:21
  674.6 79.1 %collective-permute-start.29 = (bf16[392,768]{1,0:T(8,128)(2,1)}, bf16[392,768]{1,0:T(8,128)(2,1)}, u32[]{:S(2)}, u32[]{:S(2)}) collective-permute-start(bf16[392,768]{1,0:T(8,128)(2,1)} %get-tuple-element.365), channel_id=1, source_target_pairs={{0,3},{1,0},{2,1},{3,2},{4,7},{5,4},{6,5},{7,6},{8,11},{9,8},{10,9... | collective-permute-start | bytes 1806344 | tf_op jit(solution)/shard_map/ppermute | solution.py:21
  674.7 218.1 %reduce-scatter.45.cloned.1.call-start = ((), (), s32[]{:S(2)}) async-start(), calls=%async_computation.36 | async-start | bytes 6021120 | tf_op jit(solution)/shard_map/reduce_scatter | solution.py:102
  701.1 40.6 %collective-permute-start.19 = (bf16[392,768]{1,0:T(8,128)(2,1)}, bf16[392,768]{1,0:T(8,128)(2,1)}, u32[]{:S(2)}, u32[]{:S(2)}) collective-permute-start(bf16[392,768]{1,0:T(8,128)(2,1)} %collective-permute-done.18), channel_id=1, source_target_pairs={{0,1},{1,2},{2,3},{3,0},{4,5},{5,6},{6,7},{7,4},{8,9},{9,10},{10,1... | collective-permute-start | bytes 1806344 | tf_op jit(solution)/shard_map/ppermute | solution.py:19
  704.1 49.6 %collective-permute-start.28 = (bf16[392,768]{1,0:T(8,128)(2,1)}, bf16[392,768]{1,0:T(8,128)(2,1)}, u32[]{:S(2)}, u32[]{:S(2)}) collective-permute-start(bf16[392,768]{1,0:T(8,128)(2,1)} %collective-permute-done.27), channel_id=1, source_target_pairs={{0,1},{1,2},{2,3},{3,0},{4,5},{5,6},{6,7},{7,4},{8,9},{9,10},{10,1... | collective-permute-start | bytes 1806344 | tf_op jit(solution)/shard_map/ppermute | solution.py:19
  751.6 18.7 collective-permute-start.8
  753.3 17.0 collective-permute-start.15
  753.3 23.6 %collective-permute-start.7 = (bf16[392,768]{1,0:T(8,128)(2,1)}, bf16[392,768]{1,0:T(8,128)(2,1)}, u32[]{:S(2)}, u32[]{:S(2)}) collective-permute-start(bf16[392,768]{1,0:T(8,128)(2,1)} %collective-permute-done.6), channel_id=1, source_target_pairs={{0,1},{1,2},{2,3},{3,0},{4,5},{5,6},{6,7},{7,4},{8,9},{9,10},{10,1... | collective-permute-start | bytes 1806344 | tf_op jit(solution)/shard_map/ppermute | solution.py:19
  768.9 17.0 collective-permute-start.17
  770.3 17.3 collective-permute-start.16
  844.1 99.8 %reduce-scatter.51.cloned.1.call-start = ((), (), s32[]{:S(2)}) async-start(), calls=%async_computation.39 | async-start | bytes 6021120 | tf_op jit(solution)/shard_map/reduce_scatter | solution.py:102
  851.2 143.8 %reduce-scatter.37.cloned.1.call-start = ((), (), s32[]{:S(2)}) async-start(), calls=%async_computation.32 | async-start | bytes 6021120 | tf_op jit(solution)/shard_map/reduce_scatter | solution.py:102
  868.8 177.4 %reduce-scatter.43.cloned.1.call-start = ((), (), s32[]{:S(2)}) async-start(), calls=%async_computation.35 | async-start | bytes 6021120 | tf_op jit(solution)/shard_map/reduce_scatter | solution.py:102
  1052.5 15.5 collective-permute-start.23
  1159.1 61.2 %all-to-all-start.5 = ((bf16[64,25,576]{2,1,0:T(8,128)(2,1)}), bf16[64,25,576]{2,1,0:T(8,128)(2,1)S(1)}, u32[]{:S(2)}, u32[]{:S(2)}) async-start(bf16[64,25,576]{2,1,0:T(8,128)(2,1)} %copy.260), calls=%async_computation.12 | async-start | bytes 5242880 | tf_op jit(solution)/shard_map/all_to_all | solution.py:120
  1162.7 249.9 %reduce-scatter.47.cloned.1.call-start = ((), (), s32[]{:S(2)}) async-start(), calls=%async_computation.37 | async-start | bytes 6021120 | tf_op jit(solution)/shard_map/reduce_scatter | solution.py:102
  1162.8 77.1 %collective-permute-start.30 = (bf16[392,768]{1,0:T(8,128)(2,1)}, bf16[392,768]{1,0:T(8,128)(2,1)}, u32[]{:S(2)}, u32[]{:S(2)}) collective-permute-start(bf16[392,768]{1,0:T(8,128)(2,1)} %get-tuple-element.347), channel_id=1, source_target_pairs={{0,1},{1,2},{2,3},{3,0},{4,5},{5,6},{6,7},{7,4},{8,9},{9,10},{10,1... | collective-permute-start | bytes 1806344 | tf_op jit(solution)/shard_map/ppermute | solution.py:19
  1237.8 223.5 %reduce-scatter.53.cloned.1.call-start = ((), (), s32[]{:S(2)}) async-start(), calls=%async_computation.40 | async-start | bytes 6021120 | tf_op jit(solution)/shard_map/reduce_scatter | solution.py:102
  1239.9 16.8 collective-permute-start.31
  1412.5 263.6 %reduce-scatter.55.cloned.1.call-start = ((), (), s32[]{:S(2)}) async-start(), calls=%async_computation.41 | async-start | bytes 6021120 | tf_op jit(solution)/shard_map/reduce_scatter | solution.py:102
  1468.0 15.4 collective-permute-start.35
  1541.7 134.5 %reduce-scatter.49.cloned.1.call-start = ((), (), s32[]{:S(2)}) async-start(), calls=%async_computation.38 | async-start | bytes 6021120 | tf_op jit(solution)/shard_map/reduce_scatter | solution.py:102
  1557.1 16.6 collective-permute-start.25
  1619.8 122.6 %reduce-scatter.71.cloned.1.call-start = ((), (), s32[]{:S(2)}) async-start(), calls=%async_computation.49 | async-start | bytes 884736
  1626.4 180.0 %reduce-scatter.69.cloned.1.call-start = ((), (), s32[]{:S(2)}) async-start(), calls=%async_computation.48 | async-start | bytes 2211840
  1639.8 231.9 %reduce-scatter.67.cloned.1.call-start = ((), (), s32[]{:S(2)}) async-start(), calls=%async_computation.47 | async-start | bytes 884736
  1662.0 279.5 %reduce-scatter.65.cloned.1.call-start = ((), (), s32[]{:S(2)}) async-start(), calls=%async_computation.46 | async-start | bytes 2211840
  1676.0 329.9 %reduce-scatter.61.cloned.1.call-start = ((), (), s32[]{:S(2)}) async-start(), calls=%async_computation.44 | async-start | bytes 442368
  1683.4 386.8 %reduce-scatter.63.cloned.1.call-start = ((), (), s32[]{:S(2)}) async-start(), calls=%async_computation.45 | async-start | bytes 442368
  1684.6 458.4 %reduce-scatter.59.cloned.1.call-start = ((), (), s32[]{:S(2)}) async-start(), calls=%async_computation.43 | async-start | bytes 2654208 | tf_op jit(solution)/shard_map/reduce_scatter | solution.py:131
  1691.5 524.3 %reduce-scatter.57.cloned.1.call-start = ((), (), s32[]{:S(2)}) async-start(), calls=%async_computation.42 | async-start | bytes 2654208 | tf_op jit(solution)/shard_map/reduce_scatter | solution.py:130
  (169 other events, 3330.8 us)
Sparse Core Ops, SparseCore 0:
  204.5 47.0 reduce-scatter.38
  254.2 48.5 reduce-scatter.32
  539.1 48.6 reduce-scatter.34
  668.6 68.7 reduce-scatter.40
  844.2 48.5 reduce-scatter.44
  895.2 48.5 reduce-scatter.50
  946.4 48.5 reduce-scatter.36
  997.6 48.5 reduce-scatter.42
  1238.0 49.5 reduce-scatter.46
  1412.6 48.6 reduce-scatter.52
  1541.8 52.0 reduce-scatter.54
  1619.9 49.7 reduce-scatter.48
  1673.0 63.2 reduce-scatter.70
  1739.6 66.7 reduce-scatter.68
  1809.6 62.1 reduce-scatter.66
  1875.1 66.3 reduce-scatter.64
  1944.6 61.2 reduce-scatter.60
  2009.0 61.1 reduce-scatter.62
  2074.3 68.6 reduce-scatter.58
  2146.9 68.9 reduce-scatter.56
Sparse Core Ops, SparseCore 1:
  671.2 41.8 all-gather.7
  715.1 39.5 all-gather.5
